TPU v7x, 256 devices: a whole 4x4x8 slice. The times are simulated.
256 devices in a mesh: tm: 32 (over x, y, core), row: 8 (over z).
Axes of the slice: x: 4, y: 4, z: 8, core: 2. Of those that a mesh axis runs over, the one named last changes fastest.
Arguments:
- frames_in: bfloat16 [64, 32, 64, 256], P('tm', 'row'), may hold values from -6 to 6
- cotangent: bfloat16 [64, 32, 64, 256], P('tm', 'row'), may hold values from -6 to 6
- kernel: bfloat16 [9, 256, 256], replicated, may hold values from -0.125 to 0.125
- readout: bfloat16 [256, 256], replicated, may hold values from -0.375 to 0.375
- feedthrough: float32 [256], replicated, may hold values from 0.5 to 1.5
- decay_rate: float32 [64, 256], P('tm'), may hold values from 0.05 to 1, as said below
- start_state: float32 [32, 64, 256], P('row'), may hold values from -6 to 6
Outputs:
- grad_frames: bfloat16 [64, 32, 64, 256], P('tm', 'row')
- grad_kernel: float32 [9, 256, 256], P(None, 'row')
- grad_readout: float32 [256, 256], P(None, 'row')
Inputs may be any that keep to these rules, and one draw needn't show every extreme that they name: `decay_rate`: every entry lies strictly between 0 and 1.
All inputs are finite; a program needn't handle non-finite values.
Results may differ from a plain program's by a relative error of at most 0.015.
Values may be sent and summed in bfloat16 or wider, within the bound.
No kernel may reach another device: no remote copies, remote signals or barrier semaphores. Data moves between devices by JAX's collectives and lax.ppermute only.
A program may use at most 64 MiB of HBM per device.

v0:
```python
import math
import jax
import jax.numpy as jnp
from jax import lax
from jax.sharding import PartitionSpec as P

SQRT_TWO_PI = 0.7978845608
CUBIC = 0.044715


def extended(cells, sides, width):
    for axis, dim in sides:
        count = lax.axis_size(axis)
        ends = count - 1
        head = lax.slice_in_dim(cells, 0, width, axis=dim)
        tail = lax.slice_in_dim(cells, cells.shape[dim] - width, cells.shape[dim], axis=dim)
        cells = jnp.concatenate(
            [
                lax.ppermute(tail, axis, [(i, (i + 1) % count) for i in range(ends)]),
                cells,
                lax.ppermute(head, axis, [((i + 1) % count, i) for i in range(ends)]),
            ],
            axis=dim,
        )
    return cells


def carried_in(value, axis, join, neutral, backward):
    count, mine = (lax.axis_size(axis), lax.axis_index(axis))
    pieces = jax.tree.map(lambda part: lax.all_gather(part, axis), value)
    if backward:
        pieces = jax.tree.map(lambda part: part[::-1], pieces)
        mine = count - 1 - mine
    subtotal = jax.tree.map(
        lambda part, zero: jnp.full_like(part, 0) + jnp.asarray(zero, part.dtype), value, neutral
    )

    def turn(position, subtotal):
        longer = join(subtotal, jax.tree.map(lambda part: part[position], pieces))
        return jax.tree.map(lambda new, old: jnp.where(position < mine, new, old), longer, subtotal)

    return lax.fori_loop(0, count - 1, turn, subtotal)


def gelu_slope(mixture):
    inside = SQRT_TWO_PI * (mixture + CUBIC * mixture * mixture * mixture)
    tangent = jnp.tanh(inside)
    return 0.5 * (1.0 + tangent) + 0.5 * mixture * (1.0 - tangent * tangent) * SQRT_TWO_PI * (
        1.0 + 3.0 * CUBIC * mixture * mixture
    )


def block_taps(padded, band_rows, grid_width, flipped):
    pieces = []
    for vertical in range(3):
        for lateral in range(3):
            from_top = 2 - vertical if flipped else vertical
            from_left = 2 - lateral if flipped else lateral
            pieces.append(
                padded[:, from_top : from_top + band_rows, from_left : from_left + grid_width, :]
            )
    return jnp.stack(pieces, axis=3)


def compose(earlier, later):
    return (later[0] * earlier[0], later[0] * earlier[1] + later[1])


def local(frames_in, cotangent, kernel, readout, feedthrough, decay_rate, start_state):
    frames_here, band_rows, grid_width, channels = frames_in.shape
    state_width = kernel.shape[2]
    cell_count = frames_here * band_rows * grid_width
    rimmed = extended(frames_in, (("row", 1),), 1)
    padded = jnp.pad(rimmed, ((0, 0), (0, 0), (1, 1), (0, 0)))
    input_taps = block_taps(padded, band_rows, grid_width, False).reshape(cell_count, 9 * channels)
    driven = jnp.dot(
        input_taps, kernel.reshape(9 * channels, state_width), preferred_element_type=jnp.float32
    )
    driven = driven.reshape(frames_here, band_rows, grid_width, state_width)
    gain_all = jnp.sqrt(1.0 - decay_rate * decay_rate)
    leader = (lax.axis_index("tm") == 0).astype(jnp.float32)

    def advance(carried, inputs):
        driven_now, rate_now, gain_now = inputs
        carried = rate_now * carried + gain_now * driven_now
        return (carried, carried)

    _, local_states = lax.scan(advance, start_state * leader, (driven, decay_rate, gain_all))
    through = jnp.cumprod(decay_rate, axis=0)
    identity = (
        jnp.ones((state_width,), jnp.float32),
        jnp.zeros((band_rows, grid_width, state_width), jnp.float32),
    )
    _, entering = carried_in((through[-1], local_states[-1]), "tm", compose, identity, False)
    states = local_states + through[:, None, None, :] * entering[None]
    state_bf = states.astype(jnp.bfloat16).reshape(cell_count, state_width)
    mixture = jnp.dot(state_bf, readout, preferred_element_type=jnp.float32)
    slope_bf = (
        cotangent.reshape(cell_count, channels).astype(jnp.float32) * gelu_slope(mixture)
    ).astype(jnp.bfloat16)
    pulled = lax.dot_general(
        slope_bf, readout, (((1,), (1,)), ((), ())), preferred_element_type=jnp.float32
    )
    pulled = pulled.reshape(frames_here, band_rows, grid_width, state_width)
    later_rate = jnp.concatenate([decay_rate[1:], jnp.ones((1, state_width), jnp.float32)], axis=0)

    def retreat(carried, inputs):
        pulled_now, rate_next = inputs
        carried = pulled_now + rate_next * carried
        return (carried, carried)

    _, local_adjoint = lax.scan(
        retreat,
        jnp.zeros((band_rows, grid_width, state_width), jnp.float32),
        (pulled, later_rate),
        reverse=True,
    )
    remaining = jnp.flip(jnp.cumprod(jnp.flip(later_rate, 0), axis=0), 0)
    _, arriving = carried_in(
        (through[-1], decay_rate[0][None, None, :] * local_adjoint[0]),
        "tm",
        compose,
        identity,
        True,
    )
    adjoint = local_adjoint + remaining[:, None, None, :] * arriving[None]
    grad_drive = (gain_all[:, None, None, :] * adjoint).astype(jnp.bfloat16)
    rim_adjoint = extended(grad_drive, (("row", 1),), 1)
    padded_drive = jnp.pad(rim_adjoint, ((0, 0), (0, 0), (1, 1), (0, 0)))
    output_taps = block_taps(padded_drive, band_rows, grid_width, True).reshape(
        cell_count, 9, state_width
    )
    spread = lax.dot_general(
        output_taps, kernel, (((1, 2), (0, 2)), ((), ())), preferred_element_type=jnp.float32
    )
    spread = spread.reshape(frames_here, band_rows, grid_width, channels)
    grad_frames = (spread + feedthrough * cotangent.astype(jnp.float32)).astype(jnp.bfloat16)
    kernel_term = lax.dot_general(
        input_taps,
        grad_drive.reshape(cell_count, state_width),
        (((0,), (0,)), ((), ())),
        preferred_element_type=jnp.float32,
    ).reshape(9, channels, state_width)
    readout_term = lax.dot_general(
        state_bf, slope_bf, (((0,), (0,)), ((), ())), preferred_element_type=jnp.float32
    )
    band_count = lax.axis_size("row")
    scaling = 1.0 / math.sqrt(cell_count * lax.axis_size("tm") * band_count)
    share_width = channels // band_count
    kernel_all, readout_all = lax.psum((kernel_term, readout_term), ("tm", "row"))
    offset_start = lax.axis_index("row") * share_width
    kernel_part = lax.dynamic_slice_in_dim(kernel_all, offset_start, share_width, 1)
    readout_part = lax.dynamic_slice_in_dim(readout_all, offset_start, share_width, 1)
    return (grad_frames, kernel_part * scaling, readout_part * scaling)


def solution(mesh):
    placed = (
        P("tm", "row", None, None),
        P("tm", "row", None, None),
        P(),
        P(),
        P(),
        P("tm", None),
        P("row", None, None),
    )
    return jax.shard_map(
        local,
        mesh=mesh,
        in_specs=placed,
        out_specs=(P("tm", "row", None, None), P(None, "row", None), P(None, "row")),
        check_vma=False,
    )
```

profile of v0, /device:TPU:2, one launch (start us, length us, event | category | flops | bytes accessed | tf_op | source)
XLA Modules:
  0.0 510.4 jit_solution(2149309793703916554)
XLA Ops:
  8.2 3.8 collective-permute-start
  12.1 1.3 collective-permute-start.1
  15.1 3.2 collective-permute-done.1
  23.3 24.2 %all-gather = f32[32,1,256]{2,1,0:T(1,128)S(1)} all-gather(f32[1,1,256]{2,1,0:T(1,128)S(1)} %slice_bitcast_fusion.12), channel_id=1, replica_groups=mesh['tm'=32,'row'=8] {'tm'}, dimensions={0}, use_global_device_ids=true | all-gather | bytes 33792 | tf_op jit(solution)/shard_map/all_gather | solution.py:30
  47.6 36.4 %all-gather.4.cloned.1.call-done = f32[32,4,64,256]{3,2,1,0:T(8,128)} async-done(((f32[1,4,64,256]{3,2,1,0:T(8,128)}), f32[32,4,64,256]{3,2,1,0:T(8,128)}) %all-gather.4.cloned.1.call-update) | async-done | bytes 8388624 | tf_op jit(solution)/shard_map/all_gather | solution.py:30
  84.0 36.9 %while.58 = (s32[]{:T(128)}, f32[4,64,256]{2,1,0:T(8,128)S(1)}, s32[]{:T(128)}, f32[32,256]{1,0:T(8,128)S(1)}, f32[32,4,64,256]{3,2,1,0:T(8,128)}, /*index=5*/s32[]{:T(128)}, s32[]{:T(128)}) while((s32[]{:T(128)}, f32[4,64,256]{2,1,0:T(8,128)S(1)}, s32[]{:T(128)}, f32[32,256]{1,0:T(8,128)S(1)}, f32[32,4,64,256]{3,2,1,0:T(8,128)}, ...), condition=%wide.region_4.5_spmd.clone, body=%wide.region_3.4_spmd.clone.sunk | while | flops 262148 | bytes 789609 | solution.py:42
  84.0 1.2 fusion.59
  85.2 1.1 fusion.59
  86.4 1.1 fusion.59
  87.6 1.1 fusion.59
  88.8 1.1 fusion.59
  90.0 1.1 fusion.59
  91.2 1.1 fusion.59
  92.4 1.1 fusion.59
  93.5 1.1 fusion.59
  94.7 1.1 fusion.59
  95.9 1.1 fusion.59
  97.1 1.1 fusion.59
  98.3 1.1 fusion.59
  99.5 1.1 fusion.59
  100.7 1.1 fusion.59
  101.9 1.1 fusion.59
  103.1 1.1 fusion.59
  104.3 1.1 fusion.59
  105.4 1.1 fusion.59
  106.6 1.1 fusion.59
  107.8 1.1 fusion.59
  109.0 1.1 fusion.59
  110.2 1.1 fusion.59
  111.4 1.1 fusion.59
  112.6 1.1 fusion.59
  113.8 1.1 fusion.59
  115.0 1.1 fusion.59
  116.1 1.1 fusion.59
  117.3 1.1 fusion.59
  123.2 3.3 copy.51
  126.5 2.8 copy.57
  129.3 4.3 copy.52
  134.5 45.9 %all-gather.6.cloned.1.call-done = f32[32,4,64,256]{3,2,1,0:T(8,128)} async-done(((f32[1,4,64,256]{3,2,1,0:T(8,128)}), f32[32,4,64,256]{3,2,1,0:T(8,128)}) %all-gather.6.cloned.1.call-update) | async-done | bytes 8388624 | tf_op jit(solution)/shard_map/all_gather | solution.py:30
  180.4 7.7 %rev.16 = f32[32,4,64,256]{3,2,1,0:T(8,128)} reverse(f32[32,4,64,256]{3,2,1,0:T(8,128)} %all-gather.6.cloned.1.call-done), dimensions={0} | reverse | bytes 16777216 | tf_op jit(solution)/shard_map/rev | solution.py:32
  188.1 36.8 %while.60 = (s32[]{:T(128)}, f32[4,64,256]{2,1,0:T(8,128)S(1)}, s32[]{:T(128)}, f32[32,256]{1,0:T(8,128)S(1)}, f32[32,4,64,256]{3,2,1,0:T(8,128)}, /*index=5*/s32[]{:T(128)}, s32[]{:T(128)}) while((s32[]{:T(128)}, f32[4,64,256]{2,1,0:T(8,128)S(1)}, s32[]{:T(128)}, f32[32,256]{1,0:T(8,128)S(1)}, f32[32,4,64,256]{3,2,1,0:T(8,128)}, ...), condition=%wide.region_9.10_spmd.clone, body=%wide.region_8.9_spmd.clone.sunk | while | flops 262148 | bytes 789609 | solution.py:42
  225.1 3.5 collective-permute-start.2
  228.6 1.3 collective-permute-start.3
  229.9 3.9 fusion.45
  235.9 1.5 fusion.4
  237.4 263.4 %all-reduce.6.cloned.1.call-done = (f32[9,256,256]{2,1,0:T(8,128)}, f32[256,256]{0,1:T(8,128)}) async-done(((f32[9,256,256]{2,1,0:T(8,128)}, f32[256,256]{0,1:T(8,128)}), (f32[9,256,256]{2,1,0:T(8,128)}, f32[256,256]{0,1:T(8,128)})) %all-reduce.6.cloned.1.call-update) | async-done | bytes 2621456 | tf_op jit(solution)/shard_map/psum | solution.py:150
  500.8 1.7 dynamic-slice_multiply_fusion
  502.5 1.4 dynamic-slice_multiply_fusion.1
  (176 shorter events, 52.0 us)
Async XLA Ops:
  7.2 13.5 %copy-start = (bf16[9,256,256]{2,1,0:T(8,128)(2,1)S(1)}, bf16[9,256,256]{2,1,0:T(8,128)(2,1)}, u32[]{:S(2)}) copy-start(bf16[9,256,256]{2,1,0:T(8,128)(2,1)} %param.17) | copy-start | bytes 3538948
  7.2 13.2 %copy-start.1 = (bf16[2,4,64,256]{3,2,1,0:T(8,128)(2,1)S(1)}, bf16[2,4,64,256]{3,2,1,0:T(8,128)(2,1)}, u32[]{:S(2)}) copy-start(bf16[2,4,64,256]{3,2,1,0:T(8,128)(2,1)} %param.15) | copy-start | bytes 786436
  7.2 76.8 %all-gather.4.cloned.1.call-start = ((), (), s32[]{:S(2)}) async-start(), calls=%async_computation | async-start | bytes 8650752 | tf_op jit(solution)/shard_map/all_gather | solution.py:30
  8.2 6.8 %collective-permute-start = (bf16[2,1,64,256]{3,2,1,0:T(8,128)(2,1)S(1)}, bf16[2,1,64,256]{3,2,1,0:T(8,128)(2,1)S(1)}, u32[]{:S(2)}, u32[]{:S(2)}) collective-permute-start(bf16[2,1,64,256]{3,2,1,0:T(8,128)(2,1)S(1)} %get-tuple-element.436), channel_id=1, source_target_pairs={{0,1},{1,2},{2,3},{3,4},{4,5},{5,6},{6,7},{8,9},{9,10},{10,11},{11... | collective-permute-start | bytes 196616 | tf_op jit(solution)/shard_map/ppermute | solution.py:19
  12.1 6.2 %collective-permute-start.1 = (bf16[2,1,64,256]{3,2,1,0:T(8,128)(2,1)S(1)}, bf16[2,1,64,256]{3,2,1,0:T(8,128)(2,1)S(1)}, u32[]{:S(2)}, u32[]{:S(2)}) collective-permute-start(bf16[2,1,64,256]{3,2,1,0:T(8,128)(2,1)S(1)} %get-tuple-element.437), channel_id=1, source_target_pairs={{1,0},{2,1},{3,2},{4,3},{5,4},{6,5},{7,6},{9,8},{10,9},{11,10},{12... | collective-permute-start | bytes 196616 | tf_op jit(solution)/shard_map/ppermute | solution.py:21
  20.6 1.5 copy-start.2
  20.6 1.5 copy-start.4
  23.2 157.2 %all-gather.6.cloned.1.call-start = ((), (), s32[]{:S(2)}) async-start(), calls=%async_computation.1 | async-start | bytes 8650752 | tf_op jit(solution)/shard_map/all_gather | solution.py:30
  84.0 37.0 %copy-start.3 = (bf16[256,256]{1,0:T(8,128)(2,1)S(1)}, bf16[256,256]{1,0:T(8,128)(2,1)}, u32[]{:S(2)}) copy-start(bf16[256,256]{1,0:T(8,128)(2,1)} %param.18) | copy-start | bytes 393220
  84.0 37.0 %copy-start.5 = (bf16[2,4,64,256]{3,2,1,0:T(8,128)(2,1)S(1)}, bf16[2,4,64,256]{3,2,1,0:T(8,128)(2,1)}, u32[]{:S(2)}) copy-start(bf16[2,4,64,256]{3,2,1,0:T(8,128)(2,1)} %param.16) | copy-start | bytes 786436
  122.8 378.0 %all-reduce.6.cloned.1.call-start = ((), (), s32[]{:S(2)}) async-start(), calls=%async_computation.2 | async-start | bytes 5242880 | tf_op jit(solution)/shard_map/psum | solution.py:150
  225.1 8.7 %collective-permute-start.2 = (bf16[2,1,64,256]{3,2,1,0:T(8,128)(2,1)S(1)}, bf16[2,1,64,256]{3,2,1,0:T(8,128)(2,1)S(1)}, u32[]{:S(2)}, u32[]{:S(2)}) collective-permute-start(bf16[2,1,64,256]{3,2,1,0:T(8,128)(2,1)S(1)} %get-tuple-element.434), channel_id=1, source_target_pairs={{0,1},{1,2},{2,3},{3,4},{4,5},{5,6},{6,7},{8,9},{9,10},{10,11},{11... | collective-permute-start | bytes 196616 | tf_op jit(solution)/shard_map/ppermute | solution.py:19
  228.6 6.2 %collective-permute-start.3 = (bf16[2,1,64,256]{3,2,1,0:T(8,128)(2,1)S(1)}, bf16[2,1,64,256]{3,2,1,0:T(8,128)(2,1)S(1)}, u32[]{:S(2)}, u32[]{:S(2)}) collective-permute-start(bf16[2,1,64,256]{3,2,1,0:T(8,128)(2,1)S(1)} %get-tuple-element.435), channel_id=1, source_target_pairs={{1,0},{2,1},{3,2},{4,3},{5,4},{6,5},{7,6},{9,8},{10,9},{11,10},{12... | collective-permute-start | bytes 196616 | tf_op jit(solution)/shard_map/ppermute | solution.py:21
  234.9 1.0 copy-start.6
  234.9 0.9 copy-start.7
Sparse Core Ops, SparseCore 0:
  23.3 60.6 all-gather.3
  122.9 57.4 all-gather.5
  233.9 266.8 all-reduce.5
where the time goes:
time: 513 us; the launch traced here: 510 us
  waiting for transfers between devices  350 us (68%)
  other arithmetic  79.8 us (16%)
  blocking collectives  24.2 us (5%)
  local copies, waits for them, and re-layouts  22.5 us (4%)
  between operations  14.2 us (3%)
  starting transfers between devices  9.99 us (2%)
  matrix products  7.92 us (2%)
    psum x1, waiting for transfers between devices, local(): lax.psum((kernel_term, readout_term), ('tm', 'row'))  263 us
    all_gather x2, waiting for transfers between devices, carried_in(): pieces = jax.tree.map(lambda part: lax.all_gather(part, axis), value)  82.3 us
    select_n x62, other arithmetic, turn(): jnp.where(position < mine, new, old)  71.3 us
    all_gather x1, blocking collectives, carried_in(): pieces = jax.tree.map(lambda part: lax.all_gather(part, axis), value)  24.2 us
  transfers between devices with their start and end apart: 7, of which 5 were waited for; matrix products, arithmetic and copies ran while one was open for 4% of the time, Pallas kernels for 0%

commit v1 on v0

--- a/solution.py
+++ b/solution.py
@@ -147,7 +147,7 @@
     band_count = lax.axis_size("row")
     scaling = 1.0 / math.sqrt(cell_count * lax.axis_size("tm") * band_count)
     share_width = channels // band_count
-    kernel_all, readout_all = lax.psum((kernel_term, readout_term), ("tm", "row"))
+    kernel_all, readout_all = jax.lax.psum(jax.lax.psum((kernel_term, readout_term), "row"), "tm")
     offset_start = lax.axis_index("row") * share_width
     kernel_part = lax.dynamic_slice_in_dim(kernel_all, offset_start, share_width, 1)
     readout_part = lax.dynamic_slice_in_dim(readout_all, offset_start, share_width, 1)

time: 513 us -> 448 us (0.87)
  waiting for transfers between devices: 350 us -> 276 us
    psum x1 -> x2, waiting for transfers between devices: 263 us -> 185 us  [the longest x1 113 us: local(): jax.lax.psum(jax.lax.psum((kernel_term, readout_term), 'row'), 'tm')]
  transfers between devices with their start and end apart: 7 -> 8, of which waited for: 5 -> 7; matrix products, arithmetic and copies ran while one was open for 4% -> 5% of each run, Pallas kernels for 0% -> 0%
where the time goes in v1:
time: 448 us; the launch traced here: 444 us
  waiting for transfers between devices  276 us (62%)
  other arithmetic  82 us (18%)
  local copies, waits for them, and re-layouts  26.3 us (6%)
  blocking collectives  24.2 us (5%)
  between operations  14.1 us (3%)
  starting transfers between devices  10 us (2%)
  matrix products  9.57 us (2%)
    psum x1, waiting for transfers between devices, local(): jax.lax.psum(jax.lax.psum((kernel_term, readout_term), 'row'), 'tm')  113 us
    all_gather x2, waiting for transfers between devices, carried_in(): pieces = jax.tree.map(lambda part: lax.all_gather(part, axis), value)  82.3 us
    psum x1, waiting for transfers between devices, local(): jax.lax.psum((kernel_term, readout_term), 'row')  72.8 us
    select_n x62, other arithmetic, turn(): jnp.where(position < mine, new, old)  71.3 us
    all_gather x1, blocking collectives, carried_in(): pieces = jax.tree.map(lambda part: lax.all_gather(part, axis), value)  24.2 us
  transfers between devices with their start and end apart: 8, of which 7 were waited for; matrix products, arithmetic and copies ran while one was open for 5% of the time, Pallas kernels for 0%

profile of v1, /device:TPU:2, one launch (start us, length us, event | category | flops | bytes accessed | tf_op | source)
XLA Modules:
  0.0 444.0 jit_solution(8415605560546625735)
XLA Ops:
  8.2 3.8 collective-permute-start
  12.1 1.3 collective-permute-start.1
  15.1 3.2 collective-permute-done.1
  23.3 24.2 %all-gather = f32[32,1,256]{2,1,0:T(1,128)S(1)} all-gather(f32[1,1,256]{2,1,0:T(1,128)S(1)} %slice_bitcast_fusion.12), channel_id=1, replica_groups=mesh['tm'=32,'row'=8] {'tm'}, dimensions={0}, use_global_device_ids=true | all-gather | bytes 33792 | tf_op jit(solution)/shard_map/all_gather | solution.py:30
  47.6 36.4 %all-gather.4.cloned.1.call-done = f32[32,4,64,256]{3,2,1,0:T(8,128)} async-done(((f32[1,4,64,256]{3,2,1,0:T(8,128)}), f32[32,4,64,256]{3,2,1,0:T(8,128)}) %all-gather.4.cloned.1.call-update) | async-done | bytes 8388624 | tf_op jit(solution)/shard_map/all_gather | solution.py:30
  84.0 36.9 %while.58 = (s32[]{:T(128)}, f32[4,64,256]{2,1,0:T(8,128)S(1)}, s32[]{:T(128)}, f32[32,256]{1,0:T(8,128)S(1)}, f32[32,4,64,256]{3,2,1,0:T(8,128)}, /*index=5*/s32[]{:T(128)}, s32[]{:T(128)}) while((s32[]{:T(128)}, f32[4,64,256]{2,1,0:T(8,128)S(1)}, s32[]{:T(128)}, f32[32,256]{1,0:T(8,128)S(1)}, f32[32,4,64,256]{3,2,1,0:T(8,128)}, ...), condition=%wide.region_4.5_spmd.clone, body=%wide.region_3.4_spmd.clone.sunk | while | flops 262148 | bytes 789609 | solution.py:42
  84.0 1.2 fusion.59
  85.2 1.1 fusion.59
  86.4 1.1 fusion.59
  87.6 1.1 fusion.59
  88.8 1.1 fusion.59
  90.0 1.1 fusion.59
  91.2 1.1 fusion.59
  92.4 1.1 fusion.59
  93.6 1.1 fusion.59
  94.7 1.1 fusion.59
  95.9 1.1 fusion.59
  97.1 1.1 fusion.59
  98.3 1.1 fusion.59
  99.5 1.1 fusion.59
  100.7 1.1 fusion.59
  101.9 1.1 fusion.59
  103.1 1.1 fusion.59
  104.3 1.1 fusion.59
  105.5 1.1 fusion.59
  106.6 1.1 fusion.59
  107.8 1.1 fusion.59
  109.0 1.1 fusion.59
  110.2 1.1 fusion.59
  111.4 1.1 fusion.59
  112.6 1.1 fusion.59
  113.8 1.1 fusion.59
  115.0 1.1 fusion.59
  123.2 3.3 copy.51
  126.5 2.8 copy.57
  129.3 4.3 copy.52
  134.6 45.9 %all-gather.6.cloned.1.call-done = f32[32,4,64,256]{3,2,1,0:T(8,128)} async-done(((f32[1,4,64,256]{3,2,1,0:T(8,128)}), f32[32,4,64,256]{3,2,1,0:T(8,128)}) %all-gather.6.cloned.1.call-update) | async-done | bytes 8388624 | tf_op jit(solution)/shard_map/all_gather | solution.py:30
  180.4 7.7 %rev.16 = f32[32,4,64,256]{3,2,1,0:T(8,128)} reverse(f32[32,4,64,256]{3,2,1,0:T(8,128)} %all-gather.6.cloned.1.call-done), dimensions={0} | reverse | bytes 16777216 | tf_op jit(solution)/shard_map/rev | solution.py:32
  188.2 36.8 %while.60 = (s32[]{:T(128)}, f32[4,64,256]{2,1,0:T(8,128)S(1)}, s32[]{:T(128)}, f32[32,256]{1,0:T(8,128)S(1)}, f32[32,4,64,256]{3,2,1,0:T(8,128)}, /*index=5*/s32[]{:T(128)}, s32[]{:T(128)}) while((s32[]{:T(128)}, f32[4,64,256]{2,1,0:T(8,128)S(1)}, s32[]{:T(128)}, f32[32,256]{1,0:T(8,128)S(1)}, f32[32,4,64,256]{3,2,1,0:T(8,128)}, ...), condition=%wide.region_9.10_spmd.clone, body=%wide.region_8.9_spmd.clone.sunk | while | flops 262148 | bytes 789609 | solution.py:42
  225.1 3.9 fusion.45
  229.1 3.5 collective-permute-start.2
  232.5 1.3 collective-permute-start.3
  234.4 4.3 collective-permute-done.3
  241.9 72.8 %all-reduce.10.cloned.1.call-done = (f32[9,256,256]{2,1,0:T(8,128)}, f32[256,256]{0,1:T(8,128)}) async-done(((f32[9,256,256]{2,1,0:T(8,128)}, f32[256,256]{0,1:T(8,128)}), (f32[9,256,256]{2,1,0:T(8,128)}, f32[256,256]{0,1:T(8,128)})) %all-reduce.10.cloned.1.call-update) | async-done | bytes 2621456 | tf_op jit(solution)/shard_map/psum | solution.py:150
  318.5 3.2 fusion.4
  321.7 112.7 %all-reduce.8.cloned.1.call-done = (f32[9,256,256]{2,1,0:T(8,128)}, f32[256,256]{0,1:T(8,128)}) async-done(((f32[9,256,256]{2,1,0:T(8,128)}, f32[256,256]{0,1:T(8,128)}), (f32[9,256,256]{2,1,0:T(8,128)}, f32[256,256]{0,1:T(8,128)})) %all-reduce.8.cloned.1.call-update) | async-done | bytes 2621456 | tf_op jit(solution)/shard_map/psum | solution.py:150
  434.4 1.7 dynamic-slice_multiply_fusion
  436.1 1.4 dynamic-slice_multiply_fusion.1
  (179 shorter events, 59.9 us)
Async XLA Ops:
  7.2 13.5 %copy-start = (bf16[9,256,256]{2,1,0:T(8,128)(2,1)S(1)}, bf16[9,256,256]{2,1,0:T(8,128)(2,1)}, u32[]{:S(2)}) copy-start(bf16[9,256,256]{2,1,0:T(8,128)(2,1)} %param.17) | copy-start | bytes 3538948
  7.2 13.2 %copy-start.1 = (bf16[2,4,64,256]{3,2,1,0:T(8,128)(2,1)S(1)}, bf16[2,4,64,256]{3,2,1,0:T(8,128)(2,1)}, u32[]{:S(2)}) copy-start(bf16[2,4,64,256]{3,2,1,0:T(8,128)(2,1)} %param.15) | copy-start | bytes 786436
  7.2 76.8 %all-gather.4.cloned.1.call-start = ((), (), s32[]{:S(2)}) async-start(), calls=%async_computation | async-start | bytes 8650752 | tf_op jit(solution)/shard_map/all_gather | solution.py:30
  8.2 6.8 %collective-permute-start = (bf16[2,1,64,256]{3,2,1,0:T(8,128)(2,1)S(1)}, bf16[2,1,64,256]{3,2,1,0:T(8,128)(2,1)S(1)}, u32[]{:S(2)}, u32[]{:S(2)}) collective-permute-start(bf16[2,1,64,256]{3,2,1,0:T(8,128)(2,1)S(1)} %get-tuple-element.438), channel_id=1, source_target_pairs={{0,1},{1,2},{2,3},{3,4},{4,5},{5,6},{6,7},{8,9},{9,10},{10,11},{11... | collective-permute-start | bytes 196616 | tf_op jit(solution)/shard_map/ppermute | solution.py:19
  12.1 6.2 %collective-permute-start.1 = (bf16[2,1,64,256]{3,2,1,0:T(8,128)(2,1)S(1)}, bf16[2,1,64,256]{3,2,1,0:T(8,128)(2,1)S(1)}, u32[]{:S(2)}, u32[]{:S(2)}) collective-permute-start(bf16[2,1,64,256]{3,2,1,0:T(8,128)(2,1)S(1)} %get-tuple-element.439), channel_id=1, source_target_pairs={{1,0},{2,1},{3,2},{4,3},{5,4},{6,5},{7,6},{9,8},{10,9},{11,10},{12... | collective-permute-start | bytes 196616 | tf_op jit(solution)/shard_map/ppermute | solution.py:21
  20.6 1.5 copy-start.2
  20.6 1.5 copy-start.4
  23.2 157.2 %all-gather.6.cloned.1.call-start = ((), (), s32[]{:S(2)}) async-start(), calls=%async_computation.1 | async-start | bytes 8650752 | tf_op jit(solution)/shard_map/all_gather | solution.py:30
  84.0 37.0 %copy-start.3 = (bf16[256,256]{1,0:T(8,128)(2,1)S(1)}, bf16[256,256]{1,0:T(8,128)(2,1)}, u32[]{:S(2)}) copy-start(bf16[256,256]{1,0:T(8,128)(2,1)} %param.18) | copy-start | bytes 393220
  84.0 37.0 %copy-start.5 = (bf16[2,4,64,256]{3,2,1,0:T(8,128)(2,1)S(1)}, bf16[2,4,64,256]{3,2,1,0:T(8,128)(2,1)}, u32[]{:S(2)}) copy-start(bf16[2,4,64,256]{3,2,1,0:T(8,128)(2,1)} %param.16) | copy-start | bytes 786436
  122.8 191.8 %all-reduce.10.cloned.1.call-start = ((), (), s32[]{:S(2)}) async-start(), calls=%async_computation.3 | async-start | bytes 5242880 | tf_op jit(solution)/shard_map/psum | solution.py:150
  229.0 205.4 %all-reduce.8.cloned.1.call-start = ((), (), s32[]{:S(2)}) async-start(), calls=%async_computation.2 | async-start | bytes 5242880 | tf_op jit(solution)/shard_map/psum | solution.py:150
  229.1 5.3 %collective-permute-start.2 = (bf16[2,1,64,256]{3,2,1,0:T(8,128)(2,1)S(1)}, bf16[2,1,64,256]{3,2,1,0:T(8,128)(2,1)S(1)}, u32[]{:S(2)}, u32[]{:S(2)}) collective-permute-start(bf16[2,1,64,256]{3,2,1,0:T(8,128)(2,1)S(1)} %get-tuple-element.436), channel_id=1, source_target_pairs={{0,1},{1,2},{2,3},{3,4},{4,5},{5,6},{6,7},{8,9},{9,10},{10,11},{11... | collective-permute-start | bytes 196616 | tf_op jit(solution)/shard_map/ppermute | solution.py:19
  232.5 6.2 %collective-permute-start.3 = (bf16[2,1,64,256]{3,2,1,0:T(8,128)(2,1)S(1)}, bf16[2,1,64,256]{3,2,1,0:T(8,128)(2,1)S(1)}, u32[]{:S(2)}, u32[]{:S(2)}) collective-permute-start(bf16[2,1,64,256]{3,2,1,0:T(8,128)(2,1)S(1)} %get-tuple-element.437), channel_id=1, source_target_pairs={{1,0},{2,1},{3,2},{4,3},{5,4},{6,5},{7,6},{9,8},{10,9},{11,10},{12... | collective-permute-start | bytes 196616 | tf_op jit(solution)/shard_map/ppermute | solution.py:21
  314.7 3.9 copy-start.6
  314.7 3.9 copy-start.7
Sparse Core Ops, SparseCore 0:
  23.3 60.6 all-gather.3
  123.0 57.4 all-gather.5
  229.1 85.5 all-reduce.9
  317.9 116.4 all-reduce.7
